TPU v7x, 32 devices: a whole 2x2x4 slice. The times are simulated.
32 devices in a mesh: ctx: 16 (over z, y, core), head: 2 (over x).
Axes of the slice: x: 2, y: 2, z: 4, core: 2. Of those that a mesh axis runs over, the one named last changes fastest.
Arguments:
- fine_query: bfloat16 [4096, 4096], P('ctx', 'head'), may hold values from -181 to 181
- fine_memory: bfloat16 [2, 4096, 1024], P(None, 'ctx', 'head'), may hold values from -6.5 to 6.5
- coarse_query: bfloat16 [2048, 4096], P('ctx', 'head'), may hold values from -181 to 181
- coarse_memory: bfloat16 [2, 2048, 1024], P(None, 'ctx', 'head'), may hold values from -6.5 to 6.5
- coarse_scale: int32 [2048], P('ctx'), may hold values from 0 to 7, never falling along the last dimension, each value on 1 to 512 neighbouring positions
- out_weight: bfloat16 [4096, 4096], P('head'), may hold values from -0.09375 to 0.09375
Outputs:
- fine_mixed: bfloat16 [4096, 4096], P(('ctx', 'head'))
- coarse_mixed: bfloat16 [2048, 4096], P(('ctx', 'head'))
Inputs may be any that keep to these rules, and one draw needn't show every extreme that they name: `coarse_scale`: never falls along the coarse tokens.
All inputs are finite; a program needn't handle non-finite values.
Results may differ from a plain program's by a relative error of at most 0.014.
Values may be sent and summed in bfloat16 or wider, within the bound.
A program may use at most 128 MiB of HBM per device.

v0:
```python
import math
import jax
import jax.numpy as jnp
from jax import lax
from jax.sharding import PartitionSpec as P

HD = 128
masked_score = -1e30


def attend_block(running, grouped, key_block, value_block, allowed, factor):
    running_max, running_sum, weighted = running
    scores = (
        jnp.einsum("rkgd,pkd->kgrp", grouped, key_block, preferred_element_type=jnp.float32)
        * factor
    )
    if allowed is not None:
        scores = jnp.where(allowed[None, None], scores, masked_score)
    new_max = jnp.maximum(running_max, jnp.max(scores, axis=-1))
    rescale = jnp.exp(running_max - new_max)
    shifted = jnp.exp(scores - new_max[..., None])
    running_sum = running_sum * rescale + jnp.sum(shifted, axis=-1)
    weighted = weighted * rescale[..., None] + jnp.einsum(
        "kgrp,pkd->kgrd",
        shifted.astype(jnp.bfloat16),
        value_block,
        preferred_element_type=jnp.float32,
    )
    return (new_max, running_sum, weighted)


def fold_keys(running, grouped, kv_piece, key_level, query_level, factor):
    length = kv_piece.shape[1]
    span_rows = math.gcd(length, 1024)
    block_count = length // span_rows
    groups = grouped.shape[1]
    key_blocks = kv_piece[0].reshape(block_count, span_rows, groups, -1)
    value_blocks = kv_piece[1].reshape(block_count, span_rows, groups, -1)
    if key_level is None:

        def advance(state, pieces):
            return (attend_block(state, grouped, pieces[0], pieces[1], None, factor), None)

        result, unused = lax.scan(advance, running, (key_blocks, value_blocks))
    else:
        level_blocks = key_level.reshape(block_count, span_rows)

        def advance(state, pieces):
            allowed = pieces[2][None, :] <= query_level[:, None]
            return (attend_block(state, grouped, pieces[0], pieces[1], allowed, factor), None)

        result, unused = lax.scan(advance, running, (key_blocks, value_blocks, level_blocks))
    return result


def mix_rows(attention, out_weight):
    return jnp.dot(attention, out_weight, preferred_element_type=jnp.float32)


def per_device(fine_query, fine_memory, coarse_query, coarse_memory, coarse_scale, out_weight):
    factor = HD ** (-0.5)
    groups = fine_memory.shape[2] // HD
    ratio = fine_query.shape[1] // (groups * HD)
    fine_rows = fine_query.shape[0]
    coarse_rows = coarse_query.shape[0]

    def group_rows(query):
        return query.reshape(query.shape[0], groups, ratio, HD)

    def start_state(length):
        return (
            jnp.full((groups, ratio, length), masked_score, jnp.float32),
            jnp.zeros((groups, ratio, length), jnp.float32),
            jnp.zeros((groups, ratio, length, HD), jnp.float32),
        )

    def finish(state):
        result = state[2] / state[1][..., None]
        return result.transpose(2, 0, 1, 3).reshape(result.shape[2], -1).astype(jnp.bfloat16)

    coarse_levels = coarse_scale.astype(jnp.float32)
    fine_grouped = group_rows(fine_query)
    fine_state = fold_keys(
        start_state(fine_rows),
        fine_grouped,
        lax.all_gather(fine_memory, "ctx", axis=1, tiled=True),
        None,
        None,
        factor,
    )
    whole_memory, whole_levels = (
        lax.all_gather(coarse_memory, "ctx", axis=1, tiled=True),
        lax.all_gather(
            coarse_levels.astype(jnp.bfloat16).reshape(1, -1), "ctx", axis=1, tiled=True
        ),
    )
    fine_state = fold_keys(fine_state, fine_grouped, whole_memory, None, None, factor)
    coarse_state = fold_keys(
        start_state(coarse_rows),
        group_rows(coarse_query),
        whole_memory,
        whole_levels[0].astype(jnp.float32),
        coarse_levels,
        factor,
    )
    fine_attention = finish(fine_state)
    coarse_attention = finish(coarse_state)
    fine_mixed = lax.psum_scatter(
        mix_rows(fine_attention, out_weight).astype(jnp.bfloat16),
        "head",
        scatter_dimension=0,
        tiled=True,
    )
    coarse_mixed = lax.psum_scatter(
        mix_rows(coarse_attention, out_weight).astype(jnp.bfloat16),
        "head",
        scatter_dimension=0,
        tiled=True,
    )
    return (fine_mixed, coarse_mixed)


def solution(mesh):
    placed = (
        P("ctx", "head"),
        P(None, "ctx", "head"),
        P("ctx", "head"),
        P(None, "ctx", "head"),
        P("ctx"),
        P("head", None),
    )
    return jax.shard_map(
        per_device,
        mesh=mesh,
        in_specs=placed,
        out_specs=(P(("ctx", "head"), None), P(("ctx", "head"), None)),
        check_vma=False,
    )
```

profile of v0, /device:TPU:0, one launch (start us, length us, event | category | flops | bytes accessed | tf_op | source)
XLA Modules:
  0.0 370.5 jit_solution(7867573203565260531)
XLA Ops:
  13.3 23.1 %all-gather.1 = bf16[16,1,128]{2,1,0:T(2,128)(2,1)S(1)} all-gather(bf16[1,1,128]{2,1,0:T(2,128)(2,1)S(1)} %get-tuple-element.299), channel_id=2, replica_groups=mesh['ctx'=16,'head'=2] {'ctx'}, dimensions={0}, use_global_device_ids=true | all-gather | bytes 4352 | tf_op jit(solution)/shard_map/all_gather | solution.py:93
  40.6 22.8 %all-gather.7.cloned.1.call-done = bf16[2,2048,512]{2,1,0:T(8,128)(2,1)} async-done(((bf16[2,128,512]{2,1,0:T(8,128)(2,1)}), bf16[2,2048,512]{2,1,0:T(8,128)(2,1)}) %all-gather.7.cloned.1.call-update) | async-done | bytes 4194320 | tf_op jit(solution)/shard_map/all_gather | solution.py:92
  82.3 33.2 %while.46 = (s32[]{:T(128)}, f32[4,4,128]{2,1,0:T(4,128)S(1)}, f32[4,4,128]{2,1,0:T(4,128)S(1)}, f32[4,4,128,128]{3,2,1,0:T(8,128)}, f32[2,1024]{1,0:T(2,128)S(1...) while((s32[]{:T(128)}, f32[4,4,128]{2,1,0:T(4,128)S(1)}, ...), condition=%wide.region_12.13_spmd.clone, body=%wide.region_9.12_spmd.clone.sunk | while | flops 1097738240 | bytes 64108184 | solution.py:52
  82.5 5.9 %fusion.87 = (f32[4,4,128]{2,1,0:T(4,128)S(1)}, f32[4,1024,128,4]{2,1,3,0:T(8,128)}) fusion(pred[128,1024]{0,1:T(8,128)(4,1)S(1)} %broadcast_compare_fusion.2, bf16[128,4,4,128]{3,0,2,1:T(8,128)(2,1)} %get-tuple-element.553, bf16[2,1024,4,128]{3,1,2,0:T(8,128)(2,1)} %get-tuple-element.552, s32[]{:T(128)} %get-tuple-element.535), kind=kOutput, calls=%fused_computation.43.clone.1 | convolution fusion | flops 543160320 | bytes 10101248 | tf_op jit(solution)/shard_map/while/body/eval_jaxpr/rkgd,pkd->kgrp/dot_general | solution.py:14
  99.0 5.9 %fusion.87 = (f32[4,4,128]{2,1,0:T(4,128)S(1)}, f32[4,1024,128,4]{2,1,3,0:T(8,128)}) fusion(pred[128,1024]{0,1:T(8,128)(4,1)S(1)} %broadcast_compare_fusion.2, bf16[128,4,4,128]{3,0,2,1:T(8,128)(2,1)} %get-tuple-element.553, bf16[2,1024,4,128]{3,1,2,0:T(8,128)(2,1)} %get-tuple-element.552, s32[]{:T(128)} %get-tuple-element.535), kind=kOutput, calls=%fused_computation.43.clone.1 | convolution fusion | flops 543160320 | bytes 10101248 | tf_op jit(solution)/shard_map/while/body/eval_jaxpr/rkgd,pkd->kgrp/dot_general | solution.py:14
  119.4 9.5 %convolution_convert_fusion.1 = bf16[128,4096]{1,0:T(8,128)(2,1)} fusion(bf16[128,2048]{0,1:T(8,128)(2,1)S(1)} %bitcast.155, bf16[2048,4096]{1,0:T(8,128)(2,1)} %param.17), kind=kOutput, calls=%fused_computation.64 | convolution fusion | flops 2148007936 | bytes 18350080 | tf_op jit(solution)/shard_map/dot_general | solution.py:57
  129.2 9.2 %all-gather.5.cloned.1.call-done = bf16[2,4096,512]{2,1,0:T(8,128)(2,1)} async-done(((bf16[2,256,512]{2,1,0:T(8,128)(2,1)}), bf16[2,4096,512]{2,1,0:T(8,128)(2,1)}) %all-gather.5.cloned.1.call-update) | async-done | bytes 8388624 | tf_op jit(solution)/shard_map/all_gather | solution.py:86
  138.4 5.7 %fusion.49 = (bf16[1,4096,512]{2,1,0:T(8,128)(2,1)}, bf16[1,4096,512]{2,1,0:T(8,128)(2,1)}) fusion(bf16[2,4096,512]{2,1,0:T(8,128)(2,1)} %all-gather.5.cloned.1.call-done), kind=kLoop, calls=%fused_computation.69 | loop fusion | bytes 16777216 | tf_op jit(solution)/shard_map/slice | solution.py:38
  144.1 6.9 %reshape_squeeze.14 = bf16[4,1024,4,128]{3,2,1,0:T(4,128)(2,1)} reshape(bf16[1,4096,512]{2,1,0:T(8,128)(2,1)} %get-tuple-element.295) | data formatting | bytes 8388608 | tf_op jit(solution)/shard_map/reshape;squeeze | solution.py:37
  151.1 6.9 %reshape_squeeze.15 = bf16[4,1024,4,128]{3,2,1,0:T(4,128)(2,1)} reshape(bf16[1,4096,512]{2,1,0:T(8,128)(2,1)} %get-tuple-element.294) | data formatting | bytes 8388608 | tf_op jit(solution)/shard_map/reshape;squeeze | solution.py:38
  158.0 107.8 %while.45 = (s32[]{:T(128)}, f32[4,4,256]{2,1,0:T(4,128)S(1)}, f32[4,4,256]{2,1,0:T(4,128)S(1)}, f32[4,4,256,128]{3,2,1,0:T(8,128)S(1)}, bf16[4,1024,4,128]{3,2,...) while((s32[]{:T(128)}, f32[4,4,256]{2,1,0:T(4,128)S(1)}, ...), condition=%wide.region_3.4_spmd.clone, body=%wide.region_0.3_spmd.clone.sunk | while | flops 2182631424 | bytes 66322564 | solution.py:44
  161.2 7.0 %bitcast_reduce_fusion.5 = (f32[4,4,256]{2,1,0:T(4,128)S(1)}, f32[4,1024,256,4]{2,1,3,0:T(8,128)}) fusion(bf16[256,4,4,128]{3,0,2,1:T(8,128)(2,1)S(1)} %get-tuple-element.496, bf16[1,1024,4,128]{3,2,1,0:T(4,128)(2,1)S(1)} %get-tuple-element.454), kind=kOutput, calls=%fused_computation.20.clone.1 | convolution fusion | flops 1082126336 | bytes 18890752 | tf_op jit(solution)/shard_map/while/body/eval_jaxpr/rkgd,pkd->kgrp/dot_general | solution.py:14
  168.2 8.7 %fusion.81 = f32[4,4,256]{2,1,0:T(4,128)S(1)} fusion(f32[4,1024,256,4]{2,1,3,0:T(8,128)} %get-tuple-element.456, f32[4,4,256]{2,1,0:T(4,128)S(1)} %select_maximum_fusion.4), kind=kLoop, calls=%fused_computation.23.clone.1 | loop fusion | flops 12578816 | bytes 16809984 | tf_op jit(solution)/shard_map/while/body/eval_jaxpr/reduce_sum | solution.py:22
  176.9 8.0 %fusion.83 = f32[4,4,256,128]{3,2,1,0:T(8,128)S(1)} fusion(f32[4,4,256,128]{3,2,1,0:T(8,128)S(1)} %get-tuple-element.485, f32[4,1024,256,4]{2,1,3,0:T(8,128)} %get-tuple-element.456, f32[4,4,256]{2,1,0:T(4,128)S(1)} %select_maximum_fusion.4, bf16[1,1024,4,128]{3,2,1,0:T(4,128)(2,1)S(1)} %copy-done.1, f32[4,4,256]{2,1,0:T(4,128)S(1)} %get-tuple-element.459, ...), kind=kOutput, calls=%fused_computation.28.clone.1 | convolution fusion | flops 1087897600 | bytes 22052864 | tf_op jit(solution)/shard_map/while/body/eval_jaxpr/kgrp,pkd->kgrd/dot_general | solution.py:23
  188.2 7.0 %bitcast_reduce_fusion.5 = (f32[4,4,256]{2,1,0:T(4,128)S(1)}, f32[4,1024,256,4]{2,1,3,0:T(8,128)}) fusion(bf16[256,4,4,128]{3,0,2,1:T(8,128)(2,1)S(1)} %get-tuple-element.496, bf16[1,1024,4,128]{3,2,1,0:T(4,128)(2,1)S(1)} %get-tuple-element.454), kind=kOutput, calls=%fused_computation.20.clone.1 | convolution fusion | flops 1082126336 | bytes 18890752 | tf_op jit(solution)/shard_map/while/body/eval_jaxpr/rkgd,pkd->kgrp/dot_general | solution.py:14
  195.2 8.7 %fusion.81 = f32[4,4,256]{2,1,0:T(4,128)S(1)} fusion(f32[4,1024,256,4]{2,1,3,0:T(8,128)} %get-tuple-element.456, f32[4,4,256]{2,1,0:T(4,128)S(1)} %select_maximum_fusion.4), kind=kLoop, calls=%fused_computation.23.clone.1 | loop fusion | flops 12578816 | bytes 16809984 | tf_op jit(solution)/shard_map/while/body/eval_jaxpr/reduce_sum | solution.py:22
  203.9 8.0 %fusion.83 = f32[4,4,256,128]{3,2,1,0:T(8,128)S(1)} fusion(f32[4,4,256,128]{3,2,1,0:T(8,128)S(1)} %get-tuple-element.485, f32[4,1024,256,4]{2,1,3,0:T(8,128)} %get-tuple-element.456, f32[4,4,256]{2,1,0:T(4,128)S(1)} %select_maximum_fusion.4, bf16[1,1024,4,128]{3,2,1,0:T(4,128)(2,1)S(1)} %copy-done.1, f32[4,4,256]{2,1,0:T(4,128)S(1)} %get-tuple-element.459, ...), kind=kOutput, calls=%fused_computation.28.clone.1 | convolution fusion | flops 1087897600 | bytes 22052864 | tf_op jit(solution)/shard_map/while/body/eval_jaxpr/kgrp,pkd->kgrd/dot_general | solution.py:23
  215.1 7.0 %bitcast_reduce_fusion.5 = (f32[4,4,256]{2,1,0:T(4,128)S(1)}, f32[4,1024,256,4]{2,1,3,0:T(8,128)}) fusion(bf16[256,4,4,128]{3,0,2,1:T(8,128)(2,1)S(1)} %get-tuple-element.496, bf16[1,1024,4,128]{3,2,1,0:T(4,128)(2,1)S(1)} %get-tuple-element.454), kind=kOutput, calls=%fused_computation.20.clone.1 | convolution fusion | flops 1082126336 | bytes 18890752 | tf_op jit(solution)/shard_map/while/body/eval_jaxpr/rkgd,pkd->kgrp/dot_general | solution.py:14
  222.1 8.7 %fusion.81 = f32[4,4,256]{2,1,0:T(4,128)S(1)} fusion(f32[4,1024,256,4]{2,1,3,0:T(8,128)} %get-tuple-element.456, f32[4,4,256]{2,1,0:T(4,128)S(1)} %select_maximum_fusion.4), kind=kLoop, calls=%fused_computation.23.clone.1 | loop fusion | flops 12578816 | bytes 16809984 | tf_op jit(solution)/shard_map/while/body/eval_jaxpr/reduce_sum | solution.py:22
  230.8 8.0 %fusion.83 = f32[4,4,256,128]{3,2,1,0:T(8,128)S(1)} fusion(f32[4,4,256,128]{3,2,1,0:T(8,128)S(1)} %get-tuple-element.485, f32[4,1024,256,4]{2,1,3,0:T(8,128)} %get-tuple-element.456, f32[4,4,256]{2,1,0:T(4,128)S(1)} %select_maximum_fusion.4, bf16[1,1024,4,128]{3,2,1,0:T(4,128)(2,1)S(1)} %copy-done.1, f32[4,4,256]{2,1,0:T(4,128)S(1)} %get-tuple-element.459, ...), kind=kOutput, calls=%fused_computation.28.clone.1 | convolution fusion | flops 1087897600 | bytes 22052864 | tf_op jit(solution)/shard_map/while/body/eval_jaxpr/kgrp,pkd->kgrd/dot_general | solution.py:23
  242.1 7.0 %bitcast_reduce_fusion.5 = (f32[4,4,256]{2,1,0:T(4,128)S(1)}, f32[4,1024,256,4]{2,1,3,0:T(8,128)}) fusion(bf16[256,4,4,128]{3,0,2,1:T(8,128)(2,1)S(1)} %get-tuple-element.496, bf16[1,1024,4,128]{3,2,1,0:T(4,128)(2,1)S(1)} %get-tuple-element.454), kind=kOutput, calls=%fused_computation.20.clone.1 | convolution fusion | flops 1082126336 | bytes 18890752 | tf_op jit(solution)/shard_map/while/body/eval_jaxpr/rkgd,pkd->kgrp/dot_general | solution.py:14
  249.1 8.7 %fusion.81 = f32[4,4,256]{2,1,0:T(4,128)S(1)} fusion(f32[4,1024,256,4]{2,1,3,0:T(8,128)} %get-tuple-element.456, f32[4,4,256]{2,1,0:T(4,128)S(1)} %select_maximum_fusion.4), kind=kLoop, calls=%fused_computation.23.clone.1 | loop fusion | flops 12578816 | bytes 16809984 | tf_op jit(solution)/shard_map/while/body/eval_jaxpr/reduce_sum | solution.py:22
  257.8 8.0 %fusion.83 = f32[4,4,256,128]{3,2,1,0:T(8,128)S(1)} fusion(f32[4,4,256,128]{3,2,1,0:T(8,128)S(1)} %get-tuple-element.485, f32[4,1024,256,4]{2,1,3,0:T(8,128)} %get-tuple-element.456, f32[4,4,256]{2,1,0:T(4,128)S(1)} %select_maximum_fusion.4, bf16[1,1024,4,128]{3,2,1,0:T(4,128)(2,1)S(1)} %copy-done.1, f32[4,4,256]{2,1,0:T(4,128)S(1)} %get-tuple-element.459, ...), kind=kOutput, calls=%fused_computation.28.clone.1 | convolution fusion | flops 1087897600 | bytes 22052864 | tf_op jit(solution)/shard_map/while/body/eval_jaxpr/kgrp,pkd->kgrd/dot_general | solution.py:23
  265.8 52.2 %while.44 = (s32[]{:T(128)}, f32[4,4,256]{2,1,0:T(4,128)S(1)}, f32[4,4,256]{2,1,0:T(4,128)S(1)}, f32[4,4,256,128]{3,2,1,0:T(8,128)S(1)}, bf16[2,1024,4,128]{3,1,...) while((s32[]{:T(128)}, f32[4,4,256]{2,1,0:T(4,128)S(1)}, ...), condition=%wide.region_7.8_spmd, body=%wide.region_4.7_spmd.sunk | while | flops 2182094848 | bytes 66323060 | solution.py:44
  266.0 9.3 %bitcast_reduce_fusion.4 = (f32[4,4,256]{2,1,0:T(4,128)S(1)}, f32[4,1024,256,4]{2,1,3,0:T(8,128)}) fusion(bf16[256,4,4,128]{3,0,2,1:T(8,128)(2,1)S(1)} %get-tuple-element.521, bf16[2,1024,4,128]{3,1,2,0:T(8,128)(2,1)} %get-tuple-element.520, s32[]{:T(128)} %get-tuple-element.508), kind=kOutput, calls=%fused_computation.1.clone.1 | convolution fusion | flops 1082126336 | bytes 18891264 | tf_op jit(solution)/shard_map/while/body/eval_jaxpr/rkgd,pkd->kgrp/dot_general | solution.py:14
  275.3 8.7 %fusion.78 = f32[4,4,256]{2,1,0:T(4,128)S(1)} fusion(f32[4,1024,256,4]{2,1,3,0:T(8,128)} %get-tuple-element.444, f32[4,4,256]{2,1,0:T(4,128)S(1)} %max.16), kind=kLoop, calls=%fused_computation.4.clone.1 | loop fusion | flops 12578816 | bytes 16809984 | tf_op jit(solution)/shard_map/while/body/eval_jaxpr/reduce_sum | solution.py:22
  284.1 7.9 %multiply_add_fusion.5 = f32[4,4,256,128]{3,2,1,0:T(8,128)S(1)} fusion(f32[4,4,256,128]{3,2,1,0:T(8,128)S(1)} %get-tuple-element.511, f32[4,1024,256,4]{2,1,3,0:T(8,128)} %get-tuple-element.444, f32[4,4,256]{2,1,0:T(4,128)S(1)} %max.16, bf16[2,1024,4,128]{3,1,2,0:T(8,128)(2,1)S(1)} %copy-done.2, s32[]{:T(128)} %get-tuple-element.508, ...), kind=kOutput, calls=%fused_computation.8.clone.1 | convolution fusion | flops 1087373312 | bytes 22052868 | tf_op jit(solution)/shard_map/while/body/eval_jaxpr/kgrp,pkd->kgrd/dot_general | solution.py:23
  292.0 9.3 %bitcast_reduce_fusion.4 = (f32[4,4,256]{2,1,0:T(4,128)S(1)}, f32[4,1024,256,4]{2,1,3,0:T(8,128)}) fusion(bf16[256,4,4,128]{3,0,2,1:T(8,128)(2,1)S(1)} %get-tuple-element.521, bf16[2,1024,4,128]{3,1,2,0:T(8,128)(2,1)} %get-tuple-element.520, s32[]{:T(128)} %get-tuple-element.508), kind=kOutput, calls=%fused_computation.1.clone.1 | convolution fusion | flops 1082126336 | bytes 18891264 | tf_op jit(solution)/shard_map/while/body/eval_jaxpr/rkgd,pkd->kgrp/dot_general | solution.py:14
  301.3 8.7 %fusion.78 = f32[4,4,256]{2,1,0:T(4,128)S(1)} fusion(f32[4,1024,256,4]{2,1,3,0:T(8,128)} %get-tuple-element.444, f32[4,4,256]{2,1,0:T(4,128)S(1)} %max.16), kind=kLoop, calls=%fused_computation.4.clone.1 | loop fusion | flops 12578816 | bytes 16809984 | tf_op jit(solution)/shard_map/while/body/eval_jaxpr/reduce_sum | solution.py:22
  310.0 7.9 %multiply_add_fusion.5 = f32[4,4,256,128]{3,2,1,0:T(8,128)S(1)} fusion(f32[4,4,256,128]{3,2,1,0:T(8,128)S(1)} %get-tuple-element.511, f32[4,1024,256,4]{2,1,3,0:T(8,128)} %get-tuple-element.444, f32[4,4,256]{2,1,0:T(4,128)S(1)} %max.16, bf16[2,1024,4,128]{3,1,2,0:T(8,128)(2,1)S(1)} %copy-done.2, s32[]{:T(128)} %get-tuple-element.508, ...), kind=kOutput, calls=%fused_computation.8.clone.1 | convolution fusion | flops 1087373312 | bytes 22052868 | tf_op jit(solution)/shard_map/while/body/eval_jaxpr/kgrp,pkd->kgrd/dot_general | solution.py:23
  321.6 11.6 %convolution_convert_fusion = bf16[256,4096]{1,0:T(8,128)(2,1)} fusion(bf16[256,2048]{0,1:T(8,128)(2,1)S(1)} %bitcast.153, bf16[2048,4096]{1,0:T(8,128)(2,1)} %param.17), kind=kOutput, calls=%fused_computation.63 | convolution fusion | flops 4296015872 | bytes 19922944 | tf_op jit(solution)/shard_map/dot_general | solution.py:57
  333.3 30.7 %reduce-scatter.3.cloned.1.call-done = bf16[128,4096]{1,0:T(8,128)(2,1)} async-done(((bf16[256,4096]{1,0:T(8,128)(2,1)}), bf16[128,4096]{1,0:T(8,128)(2,1)}) %reduce-scatter.3.cloned.1.call-update) | async-done | bytes 1048592 | tf_op jit(solution)/shard_map/reduce_scatter | solution.py:108
  (83 shorter events, 71.5 us)
Async XLA Ops:
  7.2 56.2 %all-gather.7.cloned.1.call-start = ((), (), s32[]{:S(2)}) async-start(), calls=%async_computation.3 | async-start | bytes 4456448 | tf_op jit(solution)/shard_map/all_gather | solution.py:92
  7.9 130.5 %all-gather.5.cloned.1.call-start = ((), (), s32[]{:S(2)}) async-start(), calls=%async_computation.2 | async-start | bytes 8912896 | tf_op jit(solution)/shard_map/all_gather | solution.py:86
  8.6 324.6 %reduce-scatter.5.cloned.1.call-start = ((), (), s32[]{:S(2)}) async-start(), calls=%async_computation.5 | async-start | bytes 1572864 | tf_op jit(solution)/shard_map/reduce_scatter | solution.py:114
  88.4 5.8 %copy-start = (f32[4,1024,128,4]{2,1,3,0:T(8,128)S(1)}, f32[4,1024,128,4]{2,1,3,0:T(8,128)}, u32[]{:S(2)}) copy-start(f32[4,1024,128,4]{2,1,3,0:T(8,128)} %get-tuple-element.470) | copy-start | bytes 25165828 | tf_op jit(solution)/shard_map/while
  104.9 5.9 %copy-start = (f32[4,1024,128,4]{2,1,3,0:T(8,128)S(1)}, f32[4,1024,128,4]{2,1,3,0:T(8,128)}, u32[]{:S(2)}) copy-start(f32[4,1024,128,4]{2,1,3,0:T(8,128)} %get-tuple-element.470) | copy-start | bytes 25165828 | tf_op jit(solution)/shard_map/while
  128.9 235.0 %reduce-scatter.3.cloned.1.call-start = ((), (), s32[]{:S(2)}) async-start(), calls=%async_computation.4 | async-start | bytes 3145728 | tf_op jit(solution)/shard_map/reduce_scatter | solution.py:108
  168.2 8.7 %copy-start.1 = (bf16[1,1024,4,128]{3,2,1,0:T(4,128)(2,1)S(1)}, bf16[1,1024,4,128]{3,2,1,0:T(4,128)(2,1)}, u32[]{:S(2)}) copy-start(bf16[1,1024,4,128]{3,2,1,0:T(4,128)(2,1)} %get-tuple-element.458) | copy-start | bytes 3145732 | tf_op jit(solution)/shard_map/while
  195.2 8.7 %copy-start.1 = (bf16[1,1024,4,128]{3,2,1,0:T(4,128)(2,1)S(1)}, bf16[1,1024,4,128]{3,2,1,0:T(4,128)(2,1)}, u32[]{:S(2)}) copy-start(bf16[1,1024,4,128]{3,2,1,0:T(4,128)(2,1)} %get-tuple-element.458) | copy-start | bytes 3145732 | tf_op jit(solution)/shard_map/while
  222.1 8.7 %copy-start.1 = (bf16[1,1024,4,128]{3,2,1,0:T(4,128)(2,1)S(1)}, bf16[1,1024,4,128]{3,2,1,0:T(4,128)(2,1)}, u32[]{:S(2)}) copy-start(bf16[1,1024,4,128]{3,2,1,0:T(4,128)(2,1)} %get-tuple-element.458) | copy-start | bytes 3145732 | tf_op jit(solution)/shard_map/while
  249.1 8.7 %copy-start.1 = (bf16[1,1024,4,128]{3,2,1,0:T(4,128)(2,1)S(1)}, bf16[1,1024,4,128]{3,2,1,0:T(4,128)(2,1)}, u32[]{:S(2)}) copy-start(bf16[1,1024,4,128]{3,2,1,0:T(4,128)(2,1)} %get-tuple-element.458) | copy-start | bytes 3145732 | tf_op jit(solution)/shard_map/while
  275.3 8.7 %copy-start.2 = (bf16[2,1024,4,128]{3,1,2,0:T(8,128)(2,1)S(1)}, bf16[2,1024,4,128]{3,1,2,0:T(8,128)(2,1)}, u32[]{:S(2)}) copy-start(bf16[2,1024,4,128]{3,1,2,0:T(8,128)(2,1)} %get-tuple-element.522) | copy-start | bytes 6291460 | tf_op jit(solution)/shard_map/while
  301.3 8.7 %copy-start.2 = (bf16[2,1024,4,128]{3,1,2,0:T(8,128)(2,1)S(1)}, bf16[2,1024,4,128]{3,1,2,0:T(8,128)(2,1)}, u32[]{:S(2)}) copy-start(bf16[2,1024,4,128]{3,1,2,0:T(8,128)(2,1)} %get-tuple-element.522) | copy-start | bytes 6291460 | tf_op jit(solution)/shard_map/while
Sparse Core Ops, SparseCore 0:
  10.2 53.1 all-gather.6
  65.5 72.8 all-gather.4
  141.2 18.9 reduce-scatter.4
  333.4 30.5 reduce-scatter.2
where the time goes:
time: 372 us; the launch traced here: 370 us
  matrix products  136 us (37%)
  other arithmetic  67.1 us (18%)
  local copies, waits for them, and re-layouts  65 us (17%)
  waiting for transfers between devices  64.2 us (17%)
  blocking collectives  23.1 us (6%)
  between operations  13.9 us (4%)
    reduce_sum x8, other arithmetic, attend_block(): running_sum = running_sum * rescale + jnp.sum(shifted, axis=-1)  62.6 us
    dot_general x8, matrix products, attend_block(): jnp.einsum('rkgd,pkd->kgrp', grouped, key_block, preferred_element_type=j...  58.3 us
    dot_general x8, matrix products, attend_block(): jnp.einsum('kgrp,pkd->kgrd', shifted.astype(jnp.bfloat16), value_block, p...  57 us
    reduce_scatter x1, waiting for transfers between devices, per_device(): lax.psum_scatter(mix_rows(fine_attention, out_weight).astype(jnp.bfloat16...  30.7 us
    all_gather x1, blocking collectives, per_device(): lax.all_gather(coarse_levels.astype(jnp.bfloat16).reshape(1, -1), 'ctx',...  23.1 us
    all_gather x1, waiting for transfers between devices, per_device(): lax.all_gather(coarse_memory, 'ctx', axis=1, tiled=True)  22.8 us
    dot_general x2, matrix products, mix_rows(): return jnp.dot(attention, out_weight, preferred_element_type=jnp.float32)  21.1 us
    dynamic_slice x4, local copies, waits for them, and re-layouts, fold_keys(): result, unused = lax.scan(advance, running, (key_blocks, value_blocks))  12.9 us
  transfers between devices with their start and end apart: 4, of which 3 were waited for; matrix products, arithmetic and copies ran while one was open for 72% of the time, Pallas kernels for 0%

commit v1 on v0

--- a/solution.py
+++ b/solution.py
@@ -90,8 +90,8 @@
     )
     whole_memory, whole_levels = (
         lax.all_gather(coarse_memory, "ctx", axis=1, tiled=True),
-        lax.all_gather(
-            coarse_levels.astype(jnp.bfloat16).reshape(1, -1), "ctx", axis=1, tiled=True
+        jnp.concatenate(
+            lax.all_gather(coarse_levels.astype(jnp.bfloat16).reshape(1, -1), "ctx"), axis=1
         ),
     )
     fine_state = fold_keys(fine_state, fine_grouped, whole_memory, None, None, factor)

time: 372 us -> 372 us (level)
  no operation moved by 1% of the time
where the time goes in v1:
time: 372 us; the launch traced here: 370 us
  matrix products  136 us (37%)
  other arithmetic  67.1 us (18%)
  local copies, waits for them, and re-layouts  65 us (17%)
  waiting for transfers between devices  64.2 us (17%)
  blocking collectives  23.1 us (6%)
  between operations  13.9 us (4%)
    reduce_sum x8, other arithmetic, attend_block(): running_sum = running_sum * rescale + jnp.sum(shifted, axis=-1)  62.6 us
    dot_general x8, matrix products, attend_block(): jnp.einsum('rkgd,pkd->kgrp', grouped, key_block, preferred_element_type=j...  58.3 us
    dot_general x8, matrix products, attend_block(): jnp.einsum('kgrp,pkd->kgrd', shifted.astype(jnp.bfloat16), value_block, p...  57 us
    reduce_scatter x1, waiting for transfers between devices, per_device(): lax.psum_scatter(mix_rows(fine_attention, out_weight).astype(jnp.bfloat16...  30.7 us
    all_gather x1, blocking collectives, per_device(): lax.all_gather(coarse_levels.astype(jnp.bfloat16).reshape(1, -1), 'ctx')  23.1 us
    all_gather x1, waiting for transfers between devices, per_device(): lax.all_gather(coarse_memory, 'ctx', axis=1, tiled=True)  22.8 us
    dot_general x2, matrix products, mix_rows(): return jnp.dot(attention, out_weight, preferred_element_type=jnp.float32)  21.1 us
    dynamic_slice x4, local copies, waits for them, and re-layouts, fold_keys(): result, unused = lax.scan(advance, running, (key_blocks, value_blocks))  12.9 us
  transfers between devices with their start and end apart: 4, of which 3 were waited for; matrix products, arithmetic and copies ran while one was open for 72% of the time, Pallas kernels for 0%

profile of v1, /device:TPU:0, one launch (start us, length us, event | category | flops | bytes accessed | tf_op | source)
XLA Modules:
  0.0 370.5 jit_solution(7867573203565260531)
XLA Ops:
  13.3 23.1 %all-gather.1 = bf16[16,1,128]{2,1,0:T(2,128)(2,1)S(1)} all-gather(bf16[1,1,128]{2,1,0:T(2,128)(2,1)S(1)} %get-tuple-element.299), channel_id=2, replica_groups=mesh['ctx'=16,'head'=2] {'ctx'}, dimensions={0}, use_global_device_ids=true | all-gather | bytes 4352 | tf_op jit(solution)/shard_map/all_gather | solution.py:94
  40.6 22.8 %all-gather.7.cloned.1.call-done = bf16[2,2048,512]{2,1,0:T(8,128)(2,1)} async-done(((bf16[2,128,512]{2,1,0:T(8,128)(2,1)}), bf16[2,2048,512]{2,1,0:T(8,128)(2,1)}) %all-gather.7.cloned.1.call-update) | async-done | bytes 4194320 | tf_op jit(solution)/shard_map/all_gather | solution.py:92
  82.3 33.2 %while.46 = (s32[]{:T(128)}, f32[4,4,128]{2,1,0:T(4,128)S(1)}, f32[4,4,128]{2,1,0:T(4,128)S(1)}, f32[4,4,128,128]{3,2,1,0:T(8,128)}, f32[2,1024]{1,0:T(2,128)S(1...) while((s32[]{:T(128)}, f32[4,4,128]{2,1,0:T(4,128)S(1)}, ...), condition=%wide.region_12.13_spmd.clone, body=%wide.region_9.12_spmd.clone.sunk | while | flops 1097738240 | bytes 64108184 | solution.py:52
  82.5 5.9 %fusion.87 = (f32[4,4,128]{2,1,0:T(4,128)S(1)}, f32[4,1024,128,4]{2,1,3,0:T(8,128)}) fusion(pred[128,1024]{0,1:T(8,128)(4,1)S(1)} %broadcast_compare_fusion.2, bf16[128,4,4,128]{3,0,2,1:T(8,128)(2,1)} %get-tuple-element.553, bf16[2,1024,4,128]{3,1,2,0:T(8,128)(2,1)} %get-tuple-element.552, s32[]{:T(128)} %get-tuple-element.535), kind=kOutput, calls=%fused_computation.43.clone.1 | convolution fusion | flops 543160320 | bytes 10101248 | tf_op jit(solution)/shard_map/while/body/eval_jaxpr/rkgd,pkd->kgrp/dot_general | solution.py:14
  99.0 5.9 %fusion.87 = (f32[4,4,128]{2,1,0:T(4,128)S(1)}, f32[4,1024,128,4]{2,1,3,0:T(8,128)}) fusion(pred[128,1024]{0,1:T(8,128)(4,1)S(1)} %broadcast_compare_fusion.2, bf16[128,4,4,128]{3,0,2,1:T(8,128)(2,1)} %get-tuple-element.553, bf16[2,1024,4,128]{3,1,2,0:T(8,128)(2,1)} %get-tuple-element.552, s32[]{:T(128)} %get-tuple-element.535), kind=kOutput, calls=%fused_computation.43.clone.1 | convolution fusion | flops 543160320 | bytes 10101248 | tf_op jit(solution)/shard_map/while/body/eval_jaxpr/rkgd,pkd->kgrp/dot_general | solution.py:14
  119.4 9.5 %convolution_convert_fusion.1 = bf16[128,4096]{1,0:T(8,128)(2,1)} fusion(bf16[128,2048]{0,1:T(8,128)(2,1)S(1)} %bitcast.155, bf16[2048,4096]{1,0:T(8,128)(2,1)} %param.17), kind=kOutput, calls=%fused_computation.64 | convolution fusion | flops 2148007936 | bytes 18350080 | tf_op jit(solution)/shard_map/dot_general | solution.py:57
  129.2 9.2 %all-gather.5.cloned.1.call-done = bf16[2,4096,512]{2,1,0:T(8,128)(2,1)} async-done(((bf16[2,256,512]{2,1,0:T(8,128)(2,1)}), bf16[2,4096,512]{2,1,0:T(8,128)(2,1)}) %all-gather.5.cloned.1.call-update) | async-done | bytes 8388624 | tf_op jit(solution)/shard_map/all_gather | solution.py:86
  138.4 5.7 %fusion.49 = (bf16[1,4096,512]{2,1,0:T(8,128)(2,1)}, bf16[1,4096,512]{2,1,0:T(8,128)(2,1)}) fusion(bf16[2,4096,512]{2,1,0:T(8,128)(2,1)} %all-gather.5.cloned.1.call-done), kind=kLoop, calls=%fused_computation.69 | loop fusion | bytes 16777216 | tf_op jit(solution)/shard_map/slice | solution.py:38
  144.1 6.9 %reshape_squeeze.14 = bf16[4,1024,4,128]{3,2,1,0:T(4,128)(2,1)} reshape(bf16[1,4096,512]{2,1,0:T(8,128)(2,1)} %get-tuple-element.295) | data formatting | bytes 8388608 | tf_op jit(solution)/shard_map/reshape;squeeze | solution.py:37
  151.1 6.9 %reshape_squeeze.15 = bf16[4,1024,4,128]{3,2,1,0:T(4,128)(2,1)} reshape(bf16[1,4096,512]{2,1,0:T(8,128)(2,1)} %get-tuple-element.294) | data formatting | bytes 8388608 | tf_op jit(solution)/shard_map/reshape;squeeze | solution.py:38
  158.0 107.8 %while.45 = (s32[]{:T(128)}, f32[4,4,256]{2,1,0:T(4,128)S(1)}, f32[4,4,256]{2,1,0:T(4,128)S(1)}, f32[4,4,256,128]{3,2,1,0:T(8,128)S(1)}, bf16[4,1024,4,128]{3,2,...) while((s32[]{:T(128)}, f32[4,4,256]{2,1,0:T(4,128)S(1)}, ...), condition=%wide.region_3.4_spmd.clone, body=%wide.region_0.3_spmd.clone.sunk | while | flops 2182631424 | bytes 66322564 | solution.py:44
  161.2 7.0 %bitcast_reduce_fusion.5 = (f32[4,4,256]{2,1,0:T(4,128)S(1)}, f32[4,1024,256,4]{2,1,3,0:T(8,128)}) fusion(bf16[256,4,4,128]{3,0,2,1:T(8,128)(2,1)S(1)} %get-tuple-element.496, bf16[1,1024,4,128]{3,2,1,0:T(4,128)(2,1)S(1)} %get-tuple-element.454), kind=kOutput, calls=%fused_computation.20.clone.1 | convolution fusion | flops 1082126336 | bytes 18890752 | tf_op jit(solution)/shard_map/while/body/eval_jaxpr/rkgd,pkd->kgrp/dot_general | solution.py:14
  168.2 8.7 %fusion.81 = f32[4,4,256]{2,1,0:T(4,128)S(1)} fusion(f32[4,1024,256,4]{2,1,3,0:T(8,128)} %get-tuple-element.456, f32[4,4,256]{2,1,0:T(4,128)S(1)} %select_maximum_fusion.4), kind=kLoop, calls=%fused_computation.23.clone.1 | loop fusion | flops 12578816 | bytes 16809984 | tf_op jit(solution)/shard_map/while/body/eval_jaxpr/reduce_sum | solution.py:22
  176.9 8.0 %fusion.83 = f32[4,4,256,128]{3,2,1,0:T(8,128)S(1)} fusion(f32[4,4,256,128]{3,2,1,0:T(8,128)S(1)} %get-tuple-element.485, f32[4,1024,256,4]{2,1,3,0:T(8,128)} %get-tuple-element.456, f32[4,4,256]{2,1,0:T(4,128)S(1)} %select_maximum_fusion.4, bf16[1,1024,4,128]{3,2,1,0:T(4,128)(2,1)S(1)} %copy-done.1, f32[4,4,256]{2,1,0:T(4,128)S(1)} %get-tuple-element.459, ...), kind=kOutput, calls=%fused_computation.28.clone.1 | convolution fusion | flops 1087897600 | bytes 22052864 | tf_op jit(solution)/shard_map/while/body/eval_jaxpr/kgrp,pkd->kgrd/dot_general | solution.py:23
  188.2 7.0 %bitcast_reduce_fusion.5 = (f32[4,4,256]{2,1,0:T(4,128)S(1)}, f32[4,1024,256,4]{2,1,3,0:T(8,128)}) fusion(bf16[256,4,4,128]{3,0,2,1:T(8,128)(2,1)S(1)} %get-tuple-element.496, bf16[1,1024,4,128]{3,2,1,0:T(4,128)(2,1)S(1)} %get-tuple-element.454), kind=kOutput, calls=%fused_computation.20.clone.1 | convolution fusion | flops 1082126336 | bytes 18890752 | tf_op jit(solution)/shard_map/while/body/eval_jaxpr/rkgd,pkd->kgrp/dot_general | solution.py:14
  195.2 8.7 %fusion.81 = f32[4,4,256]{2,1,0:T(4,128)S(1)} fusion(f32[4,1024,256,4]{2,1,3,0:T(8,128)} %get-tuple-element.456, f32[4,4,256]{2,1,0:T(4,128)S(1)} %select_maximum_fusion.4), kind=kLoop, calls=%fused_computation.23.clone.1 | loop fusion | flops 12578816 | bytes 16809984 | tf_op jit(solution)/shard_map/while/body/eval_jaxpr/reduce_sum | solution.py:22
  203.9 8.0 %fusion.83 = f32[4,4,256,128]{3,2,1,0:T(8,128)S(1)} fusion(f32[4,4,256,128]{3,2,1,0:T(8,128)S(1)} %get-tuple-element.485, f32[4,1024,256,4]{2,1,3,0:T(8,128)} %get-tuple-element.456, f32[4,4,256]{2,1,0:T(4,128)S(1)} %select_maximum_fusion.4, bf16[1,1024,4,128]{3,2,1,0:T(4,128)(2,1)S(1)} %copy-done.1, f32[4,4,256]{2,1,0:T(4,128)S(1)} %get-tuple-element.459, ...), kind=kOutput, calls=%fused_computation.28.clone.1 | convolution fusion | flops 1087897600 | bytes 22052864 | tf_op jit(solution)/shard_map/while/body/eval_jaxpr/kgrp,pkd->kgrd/dot_general | solution.py:23
  215.1 7.0 %bitcast_reduce_fusion.5 = (f32[4,4,256]{2,1,0:T(4,128)S(1)}, f32[4,1024,256,4]{2,1,3,0:T(8,128)}) fusion(bf16[256,4,4,128]{3,0,2,1:T(8,128)(2,1)S(1)} %get-tuple-element.496, bf16[1,1024,4,128]{3,2,1,0:T(4,128)(2,1)S(1)} %get-tuple-element.454), kind=kOutput, calls=%fused_computation.20.clone.1 | convolution fusion | flops 1082126336 | bytes 18890752 | tf_op jit(solution)/shard_map/while/body/eval_jaxpr/rkgd,pkd->kgrp/dot_general | solution.py:14
  222.1 8.7 %fusion.81 = f32[4,4,256]{2,1,0:T(4,128)S(1)} fusion(f32[4,1024,256,4]{2,1,3,0:T(8,128)} %get-tuple-element.456, f32[4,4,256]{2,1,0:T(4,128)S(1)} %select_maximum_fusion.4), kind=kLoop, calls=%fused_computation.23.clone.1 | loop fusion | flops 12578816 | bytes 16809984 | tf_op jit(solution)/shard_map/while/body/eval_jaxpr/reduce_sum | solution.py:22
  230.8 8.0 %fusion.83 = f32[4,4,256,128]{3,2,1,0:T(8,128)S(1)} fusion(f32[4,4,256,128]{3,2,1,0:T(8,128)S(1)} %get-tuple-element.485, f32[4,1024,256,4]{2,1,3,0:T(8,128)} %get-tuple-element.456, f32[4,4,256]{2,1,0:T(4,128)S(1)} %select_maximum_fusion.4, bf16[1,1024,4,128]{3,2,1,0:T(4,128)(2,1)S(1)} %copy-done.1, f32[4,4,256]{2,1,0:T(4,128)S(1)} %get-tuple-element.459, ...), kind=kOutput, calls=%fused_computation.28.clone.1 | convolution fusion | flops 1087897600 | bytes 22052864 | tf_op jit(solution)/shard_map/while/body/eval_jaxpr/kgrp,pkd->kgrd/dot_general | solution.py:23
  242.1 7.0 %bitcast_reduce_fusion.5 = (f32[4,4,256]{2,1,0:T(4,128)S(1)}, f32[4,1024,256,4]{2,1,3,0:T(8,128)}) fusion(bf16[256,4,4,128]{3,0,2,1:T(8,128)(2,1)S(1)} %get-tuple-element.496, bf16[1,1024,4,128]{3,2,1,0:T(4,128)(2,1)S(1)} %get-tuple-element.454), kind=kOutput, calls=%fused_computation.20.clone.1 | convolution fusion | flops 1082126336 | bytes 18890752 | tf_op jit(solution)/shard_map/while/body/eval_jaxpr/rkgd,pkd->kgrp/dot_general | solution.py:14
  249.1 8.7 %fusion.81 = f32[4,4,256]{2,1,0:T(4,128)S(1)} fusion(f32[4,1024,256,4]{2,1,3,0:T(8,128)} %get-tuple-element.456, f32[4,4,256]{2,1,0:T(4,128)S(1)} %select_maximum_fusion.4), kind=kLoop, calls=%fused_computation.23.clone.1 | loop fusion | flops 12578816 | bytes 16809984 | tf_op jit(solution)/shard_map/while/body/eval_jaxpr/reduce_sum | solution.py:22
  257.8 8.0 %fusion.83 = f32[4,4,256,128]{3,2,1,0:T(8,128)S(1)} fusion(f32[4,4,256,128]{3,2,1,0:T(8,128)S(1)} %get-tuple-element.485, f32[4,1024,256,4]{2,1,3,0:T(8,128)} %get-tuple-element.456, f32[4,4,256]{2,1,0:T(4,128)S(1)} %select_maximum_fusion.4, bf16[1,1024,4,128]{3,2,1,0:T(4,128)(2,1)S(1)} %copy-done.1, f32[4,4,256]{2,1,0:T(4,128)S(1)} %get-tuple-element.459, ...), kind=kOutput, calls=%fused_computation.28.clone.1 | convolution fusion | flops 1087897600 | bytes 22052864 | tf_op jit(solution)/shard_map/while/body/eval_jaxpr/kgrp,pkd->kgrd/dot_general | solution.py:23
  265.8 52.2 %while.44 = (s32[]{:T(128)}, f32[4,4,256]{2,1,0:T(4,128)S(1)}, f32[4,4,256]{2,1,0:T(4,128)S(1)}, f32[4,4,256,128]{3,2,1,0:T(8,128)S(1)}, bf16[2,1024,4,128]{3,1,...) while((s32[]{:T(128)}, f32[4,4,256]{2,1,0:T(4,128)S(1)}, ...), condition=%wide.region_7.8_spmd, body=%wide.region_4.7_spmd.sunk | while | flops 2182094848 | bytes 66323060 | solution.py:44
  266.0 9.3 %bitcast_reduce_fusion.4 = (f32[4,4,256]{2,1,0:T(4,128)S(1)}, f32[4,1024,256,4]{2,1,3,0:T(8,128)}) fusion(bf16[256,4,4,128]{3,0,2,1:T(8,128)(2,1)S(1)} %get-tuple-element.521, bf16[2,1024,4,128]{3,1,2,0:T(8,128)(2,1)} %get-tuple-element.520, s32[]{:T(128)} %get-tuple-element.508), kind=kOutput, calls=%fused_computation.1.clone.1 | convolution fusion | flops 1082126336 | bytes 18891264 | tf_op jit(solution)/shard_map/while/body/eval_jaxpr/rkgd,pkd->kgrp/dot_general | solution.py:14
  275.3 8.7 %fusion.78 = f32[4,4,256]{2,1,0:T(4,128)S(1)} fusion(f32[4,1024,256,4]{2,1,3,0:T(8,128)} %get-tuple-element.444, f32[4,4,256]{2,1,0:T(4,128)S(1)} %max.16), kind=kLoop, calls=%fused_computation.4.clone.1 | loop fusion | flops 12578816 | bytes 16809984 | tf_op jit(solution)/shard_map/while/body/eval_jaxpr/reduce_sum | solution.py:22
  284.1 7.9 %multiply_add_fusion.5 = f32[4,4,256,128]{3,2,1,0:T(8,128)S(1)} fusion(f32[4,4,256,128]{3,2,1,0:T(8,128)S(1)} %get-tuple-element.511, f32[4,1024,256,4]{2,1,3,0:T(8,128)} %get-tuple-element.444, f32[4,4,256]{2,1,0:T(4,128)S(1)} %max.16, bf16[2,1024,4,128]{3,1,2,0:T(8,128)(2,1)S(1)} %copy-done.2, s32[]{:T(128)} %get-tuple-element.508, ...), kind=kOutput, calls=%fused_computation.8.clone.1 | convolution fusion | flops 1087373312 | bytes 22052868 | tf_op jit(solution)/shard_map/while/body/eval_jaxpr/kgrp,pkd->kgrd/dot_general | solution.py:23
  292.0 9.3 %bitcast_reduce_fusion.4 = (f32[4,4,256]{2,1,0:T(4,128)S(1)}, f32[4,1024,256,4]{2,1,3,0:T(8,128)}) fusion(bf16[256,4,4,128]{3,0,2,1:T(8,128)(2,1)S(1)} %get-tuple-element.521, bf16[2,1024,4,128]{3,1,2,0:T(8,128)(2,1)} %get-tuple-element.520, s32[]{:T(128)} %get-tuple-element.508), kind=kOutput, calls=%fused_computation.1.clone.1 | convolution fusion | flops 1082126336 | bytes 18891264 | tf_op jit(solution)/shard_map/while/body/eval_jaxpr/rkgd,pkd->kgrp/dot_general | solution.py:14
  301.3 8.7 %fusion.78 = f32[4,4,256]{2,1,0:T(4,128)S(1)} fusion(f32[4,1024,256,4]{2,1,3,0:T(8,128)} %get-tuple-element.444, f32[4,4,256]{2,1,0:T(4,128)S(1)} %max.16), kind=kLoop, calls=%fused_computation.4.clone.1 | loop fusion | flops 12578816 | bytes 16809984 | tf_op jit(solution)/shard_map/while/body/eval_jaxpr/reduce_sum | solution.py:22
  310.0 7.9 %multiply_add_fusion.5 = f32[4,4,256,128]{3,2,1,0:T(8,128)S(1)} fusion(f32[4,4,256,128]{3,2,1,0:T(8,128)S(1)} %get-tuple-element.511, f32[4,1024,256,4]{2,1,3,0:T(8,128)} %get-tuple-element.444, f32[4,4,256]{2,1,0:T(4,128)S(1)} %max.16, bf16[2,1024,4,128]{3,1,2,0:T(8,128)(2,1)S(1)} %copy-done.2, s32[]{:T(128)} %get-tuple-element.508, ...), kind=kOutput, calls=%fused_computation.8.clone.1 | convolution fusion | flops 1087373312 | bytes 22052868 | tf_op jit(solution)/shard_map/while/body/eval_jaxpr/kgrp,pkd->kgrd/dot_general | solution.py:23
  321.6 11.6 %convolution_convert_fusion = bf16[256,4096]{1,0:T(8,128)(2,1)} fusion(bf16[256,2048]{0,1:T(8,128)(2,1)S(1)} %bitcast.153, bf16[2048,4096]{1,0:T(8,128)(2,1)} %param.17), kind=kOutput, calls=%fused_computation.63 | convolution fusion | flops 4296015872 | bytes 19922944 | tf_op jit(solution)/shard_map/dot_general | solution.py:57
  333.3 30.7 %reduce-scatter.3.cloned.1.call-done = bf16[128,4096]{1,0:T(8,128)(2,1)} async-done(((bf16[256,4096]{1,0:T(8,128)(2,1)}), bf16[128,4096]{1,0:T(8,128)(2,1)}) %reduce-scatter.3.cloned.1.call-update) | async-done | bytes 1048592 | tf_op jit(solution)/shard_map/reduce_scatter | solution.py:108
  (83 shorter events, 71.5 us)
Async XLA Ops:
  7.2 56.2 %all-gather.7.cloned.1.call-start = ((), (), s32[]{:S(2)}) async-start(), calls=%async_computation.3 | async-start | bytes 4456448 | tf_op jit(solution)/shard_map/all_gather | solution.py:92
  7.9 130.5 %all-gather.5.cloned.1.call-start = ((), (), s32[]{:S(2)}) async-start(), calls=%async_computation.2 | async-start | bytes 8912896 | tf_op jit(solution)/shard_map/all_gather | solution.py:86
  8.6 324.6 %reduce-scatter.5.cloned.1.call-start = ((), (), s32[]{:S(2)}) async-start(), calls=%async_computation.5 | async-start | bytes 1572864 | tf_op jit(solution)/shard_map/reduce_scatter | solution.py:114
  88.4 5.8 %copy-start = (f32[4,1024,128,4]{2,1,3,0:T(8,128)S(1)}, f32[4,1024,128,4]{2,1,3,0:T(8,128)}, u32[]{:S(2)}) copy-start(f32[4,1024,128,4]{2,1,3,0:T(8,128)} %get-tuple-element.470) | copy-start | bytes 25165828 | tf_op jit(solution)/shard_map/while
  104.9 5.9 %copy-start = (f32[4,1024,128,4]{2,1,3,0:T(8,128)S(1)}, f32[4,1024,128,4]{2,1,3,0:T(8,128)}, u32[]{:S(2)}) copy-start(f32[4,1024,128,4]{2,1,3,0:T(8,128)} %get-tuple-element.470) | copy-start | bytes 25165828 | tf_op jit(solution)/shard_map/while
  128.9 235.0 %reduce-scatter.3.cloned.1.call-start = ((), (), s32[]{:S(2)}) async-start(), calls=%async_computation.4 | async-start | bytes 3145728 | tf_op jit(solution)/shard_map/reduce_scatter | solution.py:108
  168.2 8.7 %copy-start.1 = (bf16[1,1024,4,128]{3,2,1,0:T(4,128)(2,1)S(1)}, bf16[1,1024,4,128]{3,2,1,0:T(4,128)(2,1)}, u32[]{:S(2)}) copy-start(bf16[1,1024,4,128]{3,2,1,0:T(4,128)(2,1)} %get-tuple-element.458) | copy-start | bytes 3145732 | tf_op jit(solution)/shard_map/while
  195.2 8.7 %copy-start.1 = (bf16[1,1024,4,128]{3,2,1,0:T(4,128)(2,1)S(1)}, bf16[1,1024,4,128]{3,2,1,0:T(4,128)(2,1)}, u32[]{:S(2)}) copy-start(bf16[1,1024,4,128]{3,2,1,0:T(4,128)(2,1)} %get-tuple-element.458) | copy-start | bytes 3145732 | tf_op jit(solution)/shard_map/while
  222.1 8.7 %copy-start.1 = (bf16[1,1024,4,128]{3,2,1,0:T(4,128)(2,1)S(1)}, bf16[1,1024,4,128]{3,2,1,0:T(4,128)(2,1)}, u32[]{:S(2)}) copy-start(bf16[1,1024,4,128]{3,2,1,0:T(4,128)(2,1)} %get-tuple-element.458) | copy-start | bytes 3145732 | tf_op jit(solution)/shard_map/while
  249.1 8.7 %copy-start.1 = (bf16[1,1024,4,128]{3,2,1,0:T(4,128)(2,1)S(1)}, bf16[1,1024,4,128]{3,2,1,0:T(4,128)(2,1)}, u32[]{:S(2)}) copy-start(bf16[1,1024,4,128]{3,2,1,0:T(4,128)(2,1)} %get-tuple-element.458) | copy-start | bytes 3145732 | tf_op jit(solution)/shard_map/while
  275.3 8.7 %copy-start.2 = (bf16[2,1024,4,128]{3,1,2,0:T(8,128)(2,1)S(1)}, bf16[2,1024,4,128]{3,1,2,0:T(8,128)(2,1)}, u32[]{:S(2)}) copy-start(bf16[2,1024,4,128]{3,1,2,0:T(8,128)(2,1)} %get-tuple-element.522) | copy-start | bytes 6291460 | tf_op jit(solution)/shard_map/while
  301.3 8.7 %copy-start.2 = (bf16[2,1024,4,128]{3,1,2,0:T(8,128)(2,1)S(1)}, bf16[2,1024,4,128]{3,1,2,0:T(8,128)(2,1)}, u32[]{:S(2)}) copy-start(bf16[2,1024,4,128]{3,1,2,0:T(8,128)(2,1)} %get-tuple-element.522) | copy-start | bytes 6291460 | tf_op jit(solution)/shard_map/while
Sparse Core Ops, SparseCore 0:
  10.2 53.1 all-gather.6
  65.5 72.8 all-gather.4
  141.2 18.9 reduce-scatter.4
  333.4 30.5 reduce-scatter.2
